TPU v7x, 32 devices: a whole 2x2x4 slice. The times are simulated.
32 devices in a mesh: group: 2 (over y), lender: 4 (over z), tensor: 4 (over x, core).
Axes of the slice: x: 2, y: 2, z: 4, core: 2. Of those that a mesh axis runs over, the one named last changes fastest.
Arguments:
- activations: bfloat16 [16, 8192], P('group', 'lender'), parts along dimension 0, may hold values from -400 to 400
- norm_gain: bfloat16 [8192], P('lender'), may hold values from 0.099609375 to 1.8984375
- w_query: bfloat16 [8192, 8192], P('lender', 'tensor'), may hold values from -0.0625 to 0.0625
- w_out: bfloat16 [8192, 8192], P('tensor', 'lender'), may hold values from -0.0625 to 0.0625
- key_pool: bfloat16 [8, 256, 128, 128], P('tensor', ('group', 'lender')), parts along dimension 1, may hold values from -800 to 800
- value_block_store: bfloat16 [8, 256, 128, 128], P('tensor', ('group', 'lender')), parts along dimension 1, may hold values from -48 to 48
- block_list: int32 [16, 8, 16], P('group', 'tensor'), parts along dimension 0, may hold values from 0 to 127, as said below
- block_slot_table: int32 [8, 256], P('tensor', 'group'), parts along dimension 1, may hold values from 0 to 127, each once within a row
- kept_len: int32 [16, 8], P('group', 'tensor'), parts along dimension 0, may hold values from 1 to 16, as said below
Outputs:
- output: bfloat16 [16, 8192], P(('group', 'tensor'), 'lender'), parts along dimension 0
There are 2 independent parts, one for each index of `group`. A program takes and returns all parts, laid end to end along the dimension named above; an argument that names none is the same for every part. Nothing has to cross between parts.
Inputs may be any that keep to these rules, and one draw needn't show every extreme that they name: `block_list`: for each KV head, no logical block appears twice among all rows' lists. `kept_len`: some row of every KV head keeps 16 blocks and some other row keeps one.
All inputs are finite; a program needn't handle non-finite values.
Results may differ from a plain program's by a relative error of at most 0.012.
The roundings to bfloat16 on the way count: a program that leaves them out, or rounds other values in their place, can miss the bound.
Values may be sent and summed in bfloat16 or wider, within the bound.
No kernel may reach another device: no remote copies, remote signals or barrier semaphores. Data moves between devices by JAX's collectives and lax.ppermute only.
A program may use at most 64 MiB of HBM per device.

v0:
```python
import jax
import jax.numpy as jnp
from jax import lax
from jax.sharding import PartitionSpec as P

D = 8192
very_low = -1e30
epsilon = 1e-05


def per_device(
    activations,
    norm_gain,
    w_query,
    w_out,
    key_pool,
    value_block_store,
    block_list,
    block_slot_table,
    kept_len,
):
    row_count = activations.shape[0]
    kv_heads = key_pool.shape[0]
    slot_count = key_pool.shape[1]
    head_dim = key_pool.shape[3]
    kept_most = block_list.shape[2]
    features = activations.astype(jnp.float32)
    squares = jnp.sum(features * features, axis=1)
    scaled = (features * norm_gain.astype(jnp.float32)).astype(jnp.bfloat16)
    partial_value = jnp.dot(scaled, w_query, preferred_element_type=jnp.float32)
    projected, square_sum = lax.psum((partial_value, squares), "lender")
    inverse = lax.rsqrt(square_sum / D + epsilon)
    query_vectors = (projected * inverse[:, None] * head_dim ** (-0.5)).astype(jnp.bfloat16)
    group_size = query_vectors.shape[1] // (kv_heads * head_dim)
    query_vectors = query_vectors.reshape(row_count, kv_heads, group_size, head_dim)
    slot_lookup_table = jnp.broadcast_to(
        block_slot_table[None], (row_count,) + block_slot_table.shape
    )
    slot_ids = jnp.take_along_axis(slot_lookup_table, block_list, axis=2)
    positions = jnp.arange(kept_most, dtype=jnp.int32)
    is_live = positions[None, None, :] < kept_len[:, :, None]
    local_slot = slot_ids - lax.axis_index("lender") * slot_count
    matches = is_live[..., None] & (
        local_slot[..., None] == jnp.arange(slot_count, dtype=jnp.int32)
    )
    owner_mask = jnp.transpose(jnp.any(matches, axis=2), (1, 2, 0))
    owner_half = owner_mask.astype(jnp.bfloat16)
    owner_full = owner_mask.astype(jnp.float32)
    used_slot = jnp.any(owner_mask, axis=2)
    picked = jnp.einsum(
        "hsr,rhgd->hsgd", owner_half, query_vectors, preferred_element_type=jnp.float32
    ).astype(jnp.bfloat16)
    scores = jnp.einsum("hsgd,hstd->hsgt", picked, key_pool, preferred_element_type=jnp.float32)
    block_best = jnp.max(scores, axis=3)
    spread = jnp.where(owner_mask[..., None], block_best[:, :, None, :], very_low)
    row_best = jnp.max(spread, axis=1)
    slot_best = jnp.max(jnp.where(owner_mask[..., None], row_best[:, None, :, :], very_low), axis=2)
    slot_best = jnp.where(used_slot[..., None], slot_best, 0.0)
    weights_full = jnp.where(
        used_slot[:, :, None, None], jnp.exp(scores - slot_best[..., None]), 0.0
    )
    slot_weight = jnp.sum(weights_full, axis=3)
    slot_value = jnp.einsum(
        "hsgt,hstd->hsgd",
        weights_full.astype(jnp.bfloat16),
        value_block_store,
        preferred_element_type=jnp.float32,
    )
    row_weight = jnp.einsum(
        "hsr,hsg->rhg", owner_full, slot_weight, precision=lax.Precision.HIGHEST
    )
    row_value = jnp.einsum(
        "hsr,hsgd->rhgd", owner_full, slot_value, precision=lax.Precision.HIGHEST
    )
    row_high = jnp.transpose(row_best, (1, 0, 2))
    lenders = lax.axis_size("lender")
    home_rows = row_count // lenders
    came_best, came_weight, came_value = (
        lax.all_to_all(row_high, "lender", split_axis=0, concat_axis=0, tiled=True),
        lax.all_to_all(row_weight, "lender", split_axis=0, concat_axis=0, tiled=True),
        lax.all_to_all(row_value, "lender", split_axis=0, concat_axis=0, tiled=True),
    )
    came_best = came_best.reshape((lenders, home_rows) + came_best.shape[1:])
    came_weight = came_weight.reshape((lenders, home_rows) + came_weight.shape[1:])
    came_value = came_value.reshape((lenders, home_rows) + came_value.shape[1:])
    highest = jnp.max(came_best, axis=0)
    factor = jnp.exp(came_best - highest[None])
    home_weight = jnp.sum(came_weight * factor, axis=0)
    home_value = jnp.sum(came_value * factor[..., None], axis=0)
    home_attended = (
        (home_value / home_weight[..., None]).astype(jnp.bfloat16).reshape(home_rows, -1)
    )
    attended = lax.all_gather(home_attended, "lender", axis=0, tiled=True)
    result = lax.psum_scatter(
        jnp.dot(attended, w_out, preferred_element_type=jnp.float32),
        "tensor",
        scatter_dimension=0,
        tiled=True,
    )
    return result.astype(jnp.bfloat16)


def solution(mesh):
    in_specs = (
        P("group", "lender"),
        P("lender"),
        P("lender", "tensor"),
        P("tensor", "lender"),
        P("tensor", ("group", "lender"), None, None),
        P("tensor", ("group", "lender"), None, None),
        P("group", "tensor", None),
        P("tensor", "group"),
        P("group", "tensor"),
    )
    out_specs = P(("group", "tensor"), "lender")
    return jax.shard_map(
        per_device, mesh=mesh, in_specs=in_specs, out_specs=out_specs, check_vma=False
    )
```

profile of v0, /device:TPU:0, one launch (start us, length us, event | category | flops | bytes accessed | tf_op | source)
XLA Modules:
  0.0 116.3 jit_solution(14642296983015357791)
XLA Ops:
  6.5 0.0 copy-start
  6.5 0.0 all-reduce.3.cloned.1.call-start
  6.6 0.8 convert_element_type.31
  7.4 5.2 %fusion.15 = f32[8,2048]{1,0:T(8,128)} fusion(bf16[2048,2048]{1,0:T(8,128)(2,1)} %param.11, bf16[8,2048]{1,0:T(8,128)(2,1)} %param.9, f32[2048]{0:T(1024)S(1)} %convert_element_type.31), kind=kOutput, calls=%fused_computation.26 | convolution fusion | flops 67158016 | bytes 8495104 | tf_op jit(solution)/shard_map/dot_general | solution.py:30
  12.7 0.0 all-reduce.3.cloned.1.call-update
  12.7 0.0 copy-done.1
  12.7 0.1 fusion.13
  12.8 0.0 copy-done.2
  12.9 0.1 reshape.57
  12.9 0.0 copy-done.3
  13.0 2.6 %gather_fusion = s32[256]{0:T(256)S(1)} fusion(s32[8,2,128]{2,1,0:T(2,128)S(1)} %broadcast_in_dim.66, s32[256]{0:T(256)S(1)} %reshape.57), kind=kCustom, calls=%fused_computation | custom fusion | bytes 5120 | tf_op jit(solution)/shard_map/jit(take_along_axis)/gather | solution.py:39
  15.6 0.1 reshape.60
  15.6 0.0 copy-done.4
  15.7 0.1 copy.48
  15.7 0.1 iota_compare_fusion.1
  15.8 13.5 %psum.15 = f32[8]{0:T(128)S(1)} all-reduce(f32[8]{0:T(128)S(1)} %fusion.13), channel_id=1, replica_groups=mesh['group'=2,'lender'=4,'tensor'=4] {'lender'}, use_global_device_ids=true, to_apply=%region_4.5 | all-reduce | flops 8 | bytes 64 | tf_op jit(solution)/shard_map/psum | solution.py:31
  29.3 0.2 fusion.10
  29.5 0.0 copy-done.5
  29.5 0.6 dynamic-slice
  30.8 19.1 %all-reduce.3.cloned.1.call-done = f32[8,2048]{1,0:T(8,128)} async-done(((f32[8,2048]{1,0:T(8,128)}), f32[8,2048]{1,0:T(8,128)}) %all-reduce.3.cloned.1.call-update) | async-done | bytes 65552 | tf_op jit(solution)/shard_map/psum | solution.py:31
  49.9 0.9 multiply_convert_fusion
  50.8 0.2 convolution_convert_fusion
  51.1 1.3 %fusion.22 = (f32[2,32,8]{2,1,0:T(8,128)S(1)}, f32[2,32,8,128]{3,2,1,0:T(8,128)S(1)}) fusion(bf16[2,32,128,128]{3,2,1,0:T(8,128)(2,1)S(1)} %copy-done, bf16[2,32,8,128]{3,1,2,0:T(8,128)(2,1)S(1)} %convolution_convert_fusion), kind=kOutput, calls=%fused_computation.43 | convolution fusion | flops 16842240 | bytes 2492416 | tf_op jit(solution)/shard_map/hsgd,hstd->hsgt/dot_general | solution.py:53
  52.3 0.1 copy.52
  52.4 0.1 select_reduce_fusion.1
  52.5 0.1 select_reduce_fusion
  52.6 0.1 copy.53
  52.7 0.6 copy.57
  53.3 3.4 %all-to-all-start.1 = ((f32[8,2,8]{2,1,0:T(2,128)}), f32[8,2,8]{2,1,0:T(2,128)S(1)}, u32[]{:S(2)}, u32[]{:S(2)}) async-start(f32[8,2,8]{2,1,0:T(2,128)} %copy.57), calls=%async_computation.1 | async-start | bytes 16384 | tf_op jit(solution)/shard_map/all_to_all | solution.py:79
  56.7 0.3 fusion.1
  57.0 2.3 %fusion.3 = f32[2,32,8,128]{3,2,1,0:T(8,128)S(1)} fusion(bf16[2,32,128,128]{3,2,1,0:T(8,128)(2,1)} %param.14, f32[2,32,8,128]{3,2,1,0:T(8,128)S(1)} %get-tuple-element.8, f32[2,32,8]{2,1,0:T(8,128)S(1)} %copy.53, pred[2,32]{1,0:T(4,128)(4,1)S(1)} %bitcast_reduce_fusion), kind=kOutput, calls=%fused_computation.8 | convolution fusion | flops 16973824 | bytes 2623552 | tf_op jit(solution)/shard_map/hsgt,hstd->hsgd/dot_general | solution.py:63
  59.3 0.2 convolution_bitcast_fusion.1
  59.5 0.7 copy.63
  60.2 2.1 %all-to-all-done.1 = f32[8,2,8]{2,1,0:T(2,128)S(1)} async-done(((f32[8,2,8]{2,1,0:T(2,128)}), f32[8,2,8]{2,1,0:T(2,128)S(1)}, u32[]{:S(2)}, u32[]{:S(2)}) %all-to-all-start.1) | async-done | bytes 544 | tf_op jit(solution)/shard_map/all_to_all | solution.py:79
  62.3 3.2 %all-to-all-start.2 = ((f32[8,2,8]{2,1,0:T(2,128)}), f32[8,2,8]{2,1,0:T(2,128)S(1)}, u32[]{:S(2)}, u32[]{:S(2)}) async-start(f32[8,2,8]{2,1,0:T(2,128)} %copy.63), calls=%async_computation.2 | async-start | bytes 16384 | tf_op jit(solution)/shard_map/all_to_all | solution.py:80
  65.5 0.2 convolution_bitcast_fusion
  65.8 0.6 copy.56
  66.4 4.7 %all-to-all-done.2 = f32[8,2,8]{2,1,0:T(2,128)S(1)} async-done(((f32[8,2,8]{2,1,0:T(2,128)}), f32[8,2,8]{2,1,0:T(2,128)S(1)}, u32[]{:S(2)}, u32[]{:S(2)}) %all-to-all-start.2) | async-done | bytes 544 | tf_op jit(solution)/shard_map/all_to_all | solution.py:80
  71.1 3.3 %all-to-all-start = ((f32[8,2,8,128]{3,2,1,0:T(8,128)}), f32[8,2,8,128]{3,2,1,0:T(8,128)S(1)}, u32[]{:S(2)}, u32[]{:S(2)}) async-start(f32[8,2,8,128]{3,2,1,0:T(8,128)} %copy.56), calls=%async_computation | async-start | bytes 131072 | tf_op jit(solution)/shard_map/all_to_all | solution.py:81
  74.4 0.1 copy.59
  74.6 0.1 copy.65
  74.6 5.5 %all-to-all-done = f32[8,2,8,128]{3,2,1,0:T(8,128)S(1)} async-done(((f32[8,2,8,128]{3,2,1,0:T(8,128)}), f32[8,2,8,128]{3,2,1,0:T(8,128)S(1)}, u32[]{:S(2)}, u32[]{:S(2)}) %all-to-all-start) | async-done | bytes 65568 | tf_op jit(solution)/shard_map/all_to_all | solution.py:81
  80.2 0.1 fusion.14
  80.3 0.1 divide_convert_fusion
  80.4 13.1 %all-gather = bf16[4,2,2048]{2,1,0:T(2,128)(2,1)S(1)} all-gather(bf16[1,2,2048]{2,1,0:T(2,128)(2,1)S(1)} %bitcast.37), channel_id=1, replica_groups=mesh['group'=2,'lender'=4,'tensor'=4] {'lender'}, dimensions={0}, use_global_device_ids=true | all-gather | bytes 40960 | tf_op jit(solution)/shard_map/all_gather | solution.py:93
  93.6 4.6 %fusion.23 = f32[8,2048]{1,0:T(8,128)S(1)} fusion(bf16[8,2048]{1,0:T(8,128)(2,1)S(1)} %reshape.69, bf16[2048,2048]{1,0:T(8,128)(2,1)} %param.12), kind=kOutput, calls=%fused_computation.44 | convolution fusion | flops 67108864 | bytes 8486912 | tf_op jit(solution)/shard_map/dot_general | solution.py:95
  98.2 10.7 %all-reduce = bf16[8,2048]{1,0:T(8,128)(2,1)S(1)} all-reduce(f32[8,2048]{1,0:T(8,128)S(1)} %fusion.23), channel_id=2, replica_groups=mesh['group'=2,'lender'=4,'tensor'=4] {'tensor'}, use_global_device_ids=true, to_apply=%region_12.13.clone | all-reduce | flops 16384 | bytes 98304
  108.8 0.6 dynamic-slice_convert_fusion
  (18 shorter events, 0.2 us)
Async XLA Ops:
  6.5 44.5 %copy-start = (bf16[2,32,128,128]{3,2,1,0:T(8,128)(2,1)S(1)}, bf16[2,32,128,128]{3,2,1,0:T(8,128)(2,1)}, u32[]{:S(2)}) copy-start(bf16[2,32,128,128]{3,2,1,0:T(8,128)(2,1)} %param.13) | copy-start | bytes 6291460
  6.5 6.2 %copy-start.1 = (bf16[8,2048]{1,0:T(8,128)(2,1)S(1)}, bf16[8,2048]{1,0:T(8,128)(2,1)}, u32[]{:S(2)}) copy-start(bf16[8,2048]{1,0:T(8,128)(2,1)} %param.9) | copy-start | bytes 98308
  6.5 6.3 %copy-start.2 = (s32[8,2,16]{2,1,0:T(2,128)S(1)}, s32[8,2,16]{2,1,0:T(2,128)}, u32[]{:S(2)}) copy-start(s32[8,2,16]{2,1,0:T(2,128)} %param.15) | copy-start | bytes 3076
  6.5 6.4 %copy-start.3 = (s32[2,128]{1,0:T(2,128)S(1)}, s32[2,128]{1,0:T(2,128)}, u32[]{:S(2)}) copy-start(s32[2,128]{1,0:T(2,128)} %param.16) | copy-start | bytes 3076
  6.5 43.4 %all-reduce.3.cloned.1.call-start = ((), (), s32[]{:S(2)}) async-start(), calls=%async_computation.3 | async-start | bytes 131072 | tf_op jit(solution)/shard_map/psum | solution.py:31
  7.4 8.2 %copy-start.4 = (s32[8,2]{0,1:T(2,128)S(1)}, s32[8,2]{0,1:T(2,128)}, u32[]{:S(2)}) copy-start(s32[8,2]{0,1:T(2,128)} %param.17) | copy-start | bytes 196
  7.4 22.1 %copy-start.5 = (u32[32]{0:T(128)S(1)}, u32[32]{0:T(128)}, u32[]{:S(2)}) copy-start(u32[32]{0:T(128)} %constant.64) | copy-start | bytes 388
  53.3 9.0 %all-to-all-start.1 = ((f32[8,2,8]{2,1,0:T(2,128)}), f32[8,2,8]{2,1,0:T(2,128)S(1)}, u32[]{:S(2)}, u32[]{:S(2)}) async-start(f32[8,2,8]{2,1,0:T(2,128)} %copy.57), calls=%async_computation.1 | async-start | bytes 16384 | tf_op jit(solution)/shard_map/all_to_all | solution.py:79
  62.3 8.8 %all-to-all-start.2 = ((f32[8,2,8]{2,1,0:T(2,128)}), f32[8,2,8]{2,1,0:T(2,128)S(1)}, u32[]{:S(2)}, u32[]{:S(2)}) async-start(f32[8,2,8]{2,1,0:T(2,128)} %copy.63), calls=%async_computation.2 | async-start | bytes 16384 | tf_op jit(solution)/shard_map/all_to_all | solution.py:80
  71.1 9.1 %all-to-all-start = ((f32[8,2,8,128]{3,2,1,0:T(8,128)}), f32[8,2,8,128]{3,2,1,0:T(8,128)S(1)}, u32[]{:S(2)}, u32[]{:S(2)}) async-start(f32[8,2,8,128]{3,2,1,0:T(8,128)} %copy.56), calls=%async_computation | async-start | bytes 131072 | tf_op jit(solution)/shard_map/all_to_all | solution.py:81
Sparse Core Ops, SparseCore 0:
  12.8 37.0 all-reduce.2
where the time goes:
time: 117 us; the launch traced here: 116 us
  blocking collectives  37.3 us (32%)
  waiting for transfers between devices  31.5 us (27%)
  between operations  14.2 us (12%)
  matrix products  14 us (12%)
  starting transfers between devices  9.94 us (8%)
  local copies, waits for them, and re-layouts  6.38 us (5%)
  other arithmetic  2.96 us (3%)
    psum x1, waiting for transfers between devices, per_device(): projected, square_sum = lax.psum((partial_value, squares), 'lender')  19.1 us
    psum x1, blocking collectives, per_device(): projected, square_sum = lax.psum((partial_value, squares), 'lender')  13.5 us
    all_gather x1, blocking collectives, per_device(): attended = lax.all_gather(home_attended, 'lender', axis=0, tiled=True)  13.1 us
    unnamed x1, blocking collectives  10.7 us
    all_to_all x1, waiting for transfers between devices, per_device(): lax.all_to_all(row_value, 'lender', split_axis=0, concat_axis=0, tiled=True)  5.54 us
    dot_general x1, matrix products, per_device(): partial_value = jnp.dot(scaled, w_query, preferred_element_type=jnp.float32)  5.24 us
    all_to_all x1, waiting for transfers between devices, per_device(): lax.all_to_all(row_weight, 'lender', split_axis=0, concat_axis=0, tiled=T...  4.68 us
    dot_general x1, matrix products, per_device(): jnp.dot(attended, w_out, preferred_element_type=jnp.float32)  4.57 us
  transfers between devices with their start and end apart: 4, of which 4 were waited for; matrix products, arithmetic and copies ran while one was open for 7% of the time, Pallas kernels for 0%

commit v1 on v0

--- a/solution.py
+++ b/solution.py
@@ -1,11 +1,29 @@
+import functools
 import jax
 import jax.numpy as jnp
 from jax import lax
 from jax.sharding import PartitionSpec as P
+from jax.lax import axis_index, axis_size, ppermute
 
 D = 8192
 very_low = -1e30
 epsilon = 1e-05
+
+
+def press_lane_all(frame_in, dim_i):
+    formed = axis_size("lender")
+    v_now, inter = (formed, axis_index("lender"))
+    u_next, later = (frame_in, 1)
+    while later < v_now:
+        b_next = ppermute(u_next, "lender", tuple(((at, at ^ later) for at in range(v_now))))
+        built = jnp.concatenate([u_next, b_next], axis=dim_i)
+        mid_arr = jnp.concatenate([b_next, u_next], axis=dim_i)
+        u_next = jnp.where(inter & later == 0, built, mid_arr)
+        later = 2 * later
+    return u_next
+
+
+load_vector = functools.partial(press_lane_all, dim_i=0)
 
 
 def per_device(
@@ -90,7 +108,7 @@
     home_attended = (
         (home_value / home_weight[..., None]).astype(jnp.bfloat16).reshape(home_rows, -1)
     )
-    attended = lax.all_gather(home_attended, "lender", axis=0, tiled=True)
+    attended = load_vector(home_attended)
     result = lax.psum_scatter(
         jnp.dot(attended, w_out, preferred_element_type=jnp.float32),
         "tensor",

time: 117 us -> 112 us (0.957)
  blocking collectives: 37.3 us -> 24.1 us
  waiting for transfers between devices: 31.5 us -> 38 us
  starting transfers between devices: 9.94 us -> 11.7 us
    all_gather x1 -> x0, blocking collectives: 13.1 us -> none  [per_device(): attended = lax.all_gather(home_attended, 'lender', axis=0, tiled=True)]
    ppermute x0 -> x2, waiting for transfers between devices: none -> 5.4 us  [press_lane_all(): ppermute(u_next, 'lender', tuple(((at, at ^ later) for at in range(v_now))))]
    ppermute x0 -> x2, starting transfers between devices: none -> 1.78 us  [press_lane_all(): ppermute(u_next, 'lender', tuple(((at, at ^ later) for at in range(v_now))))]
    psum x1, waiting for transfers between devices: 19.1 us -> 20.3 us  [per_device(): projected, square_sum = lax.psum((partial_value, squares), 'lender')]
  transfers between devices with their start and end apart: 4 -> 6, of which waited for: 4 -> 6; matrix products, arithmetic and copies ran while one was open for 7% -> 8% of each run, Pallas kernels for 0% -> 0%
where the time goes in v1:
time: 112 us; the launch traced here: 111 us
  waiting for transfers between devices  38 us (34%)
  blocking collectives  24.1 us (22%)
  between operations  14.2 us (13%)
  matrix products  14 us (12%)
  starting transfers between devices  11.7 us (10%)
  local copies, waits for them, and re-layouts  6.36 us (6%)
  other arithmetic  2.99 us (3%)
    psum x1, waiting for transfers between devices, per_device(): projected, square_sum = lax.psum((partial_value, squares), 'lender')  20.3 us
    psum x1, blocking collectives, per_device(): projected, square_sum = lax.psum((partial_value, squares), 'lender')  13.5 us
    unnamed x1, blocking collectives  10.7 us
    all_to_all x1, waiting for transfers between devices, per_device(): lax.all_to_all(row_value, 'lender', split_axis=0, concat_axis=0, tiled=True)  5.46 us
    ppermute x2, waiting for transfers between devices, press_lane_all(): ppermute(u_next, 'lender', tuple(((at, at ^ later) for at in range(v_now))))  5.4 us
    dot_general x1, matrix products, per_device(): partial_value = jnp.dot(scaled, w_query, preferred_element_type=jnp.float32)  5.21 us
    all_to_all x1, waiting for transfers between devices, per_device(): lax.all_to_all(row_weight, 'lender', split_axis=0, concat_axis=0, tiled=T...  4.68 us
    dot_general x1, matrix products, per_device(): jnp.dot(attended, w_out, preferred_element_type=jnp.float32)  4.57 us
  transfers between devices with their start and end apart: 6, of which 6 were waited for; matrix products, arithmetic and copies ran while one was open for 8% of the time, Pallas kernels for 0%

profile of v1, /device:TPU:0, one launch (start us, length us, event | category | flops | bytes accessed | tf_op | source)
XLA Modules:
  0.0 111.4 jit_solution(6589503035312834621)
XLA Ops:
  6.5 0.0 all-reduce.3.cloned.1.call-start
  6.6 0.8 convert_element_type.31
  7.4 5.2 %fusion.15 = f32[8,2048]{1,0:T(8,128)} fusion(bf16[2048,2048]{1,0:T(8,128)(2,1)} %param.11, bf16[8,2048]{1,0:T(8,128)(2,1)} %param.9, f32[2048]{0:T(1024)S(1)} %convert_element_type.31), kind=kOutput, calls=%fused_computation.26 | convolution fusion | flops 67158016 | bytes 8495104 | tf_op jit(solution)/shard_map/dot_general | solution.py:48
  12.6 0.0 all-reduce.3.cloned.1.call-update
  12.7 0.0 copy-done.1
  12.7 0.1 fusion.13
  12.8 0.1 reshape.57
  12.9 0.0 copy-done.3
  12.9 0.1 copy.48
  13.0 0.1 iota_compare_fusion.1
  13.1 2.6 %gather_fusion = s32[256]{0:T(256)S(1)} fusion(s32[8,2,128]{2,1,0:T(2,128)S(1)} %broadcast_in_dim.66, s32[256]{0:T(256)S(1)} %reshape.57), kind=kCustom, calls=%fused_computation | custom fusion | bytes 5120 | tf_op jit(solution)/shard_map/jit(take_along_axis)/gather | solution.py:57
  15.7 0.1 reshape.60
  15.8 13.5 %psum.15 = f32[8]{0:T(128)S(1)} all-reduce(f32[8]{0:T(128)S(1)} %fusion.13), channel_id=1, replica_groups=mesh['group'=2,'lender'=4,'tensor'=4] {'lender'}, use_global_device_ids=true, to_apply=%region_4.5 | all-reduce | flops 8 | bytes 64 | tf_op jit(solution)/shard_map/psum | solution.py:49
  29.3 0.2 fusion.10
  29.5 20.3 %all-reduce.3.cloned.1.call-done = f32[8,2048]{1,0:T(8,128)} async-done(((f32[8,2048]{1,0:T(8,128)}), f32[8,2048]{1,0:T(8,128)}) %all-reduce.3.cloned.1.call-update) | async-done | bytes 65552 | tf_op jit(solution)/shard_map/psum | solution.py:49
  49.9 0.9 multiply_convert_fusion
  50.8 0.2 convolution_convert_fusion
  51.0 1.3 %fusion.30 = (f32[2,32,8]{2,1,0:T(8,128)S(1)}, f32[2,32,8,128]{3,2,1,0:T(8,128)S(1)}) fusion(bf16[2,32,128,128]{3,2,1,0:T(8,128)(2,1)S(1)} %copy-done, bf16[2,32,8,128]{3,1,2,0:T(8,128)(2,1)S(1)} %convolution_convert_fusion), kind=kOutput, calls=%fused_computation.53 | convolution fusion | flops 16842240 | bytes 2492416 | tf_op jit(solution)/shard_map/hsgd,hstd->hsgt/dot_general | solution.py:71
  52.3 0.1 copy.52
  52.4 0.1 select_reduce_fusion.1
  52.5 0.1 select_reduce_fusion
  52.6 0.1 copy.53
  52.7 0.6 copy.57
  53.3 3.4 %all-to-all-start.1 = ((f32[8,2,8]{2,1,0:T(2,128)}), f32[8,2,8]{2,1,0:T(2,128)S(1)}, u32[]{:S(2)}, u32[]{:S(2)}) async-start(f32[8,2,8]{2,1,0:T(2,128)} %copy.57), calls=%async_computation.1 | async-start | bytes 16384 | tf_op jit(solution)/shard_map/all_to_all | solution.py:97
  56.6 0.3 fusion.1
  57.0 2.3 %fusion.3 = f32[2,32,8,128]{3,2,1,0:T(8,128)S(1)} fusion(bf16[2,32,128,128]{3,2,1,0:T(8,128)(2,1)} %param.14, f32[2,32,8,128]{3,2,1,0:T(8,128)S(1)} %get-tuple-element.8, f32[2,32,8]{2,1,0:T(8,128)S(1)} %copy.53, pred[2,32]{1,0:T(4,128)(4,1)S(1)} %bitcast_reduce_fusion), kind=kOutput, calls=%fused_computation.8 | convolution fusion | flops 16973824 | bytes 2623552 | tf_op jit(solution)/shard_map/hsgt,hstd->hsgd/dot_general | solution.py:81
  59.3 0.2 convolution_bitcast_fusion.1
  59.5 0.7 copy.63
  60.1 2.1 %all-to-all-done.1 = f32[8,2,8]{2,1,0:T(2,128)S(1)} async-done(((f32[8,2,8]{2,1,0:T(2,128)}), f32[8,2,8]{2,1,0:T(2,128)S(1)}, u32[]{:S(2)}, u32[]{:S(2)}) %all-to-all-start.1) | async-done | bytes 544 | tf_op jit(solution)/shard_map/all_to_all | solution.py:97
  62.2 3.2 %all-to-all-start.2 = ((f32[8,2,8]{2,1,0:T(2,128)}), f32[8,2,8]{2,1,0:T(2,128)S(1)}, u32[]{:S(2)}, u32[]{:S(2)}) async-start(f32[8,2,8]{2,1,0:T(2,128)} %copy.63), calls=%async_computation.2 | async-start | bytes 16384 | tf_op jit(solution)/shard_map/all_to_all | solution.py:98
  65.5 0.2 convolution_bitcast_fusion
  65.7 0.6 copy.56
  66.4 4.7 %all-to-all-done.2 = f32[8,2,8]{2,1,0:T(2,128)S(1)} async-done(((f32[8,2,8]{2,1,0:T(2,128)}), f32[8,2,8]{2,1,0:T(2,128)S(1)}, u32[]{:S(2)}, u32[]{:S(2)}) %all-to-all-start.2) | async-done | bytes 544 | tf_op jit(solution)/shard_map/all_to_all | solution.py:98
  71.0 3.3 %all-to-all-start = ((f32[8,2,8,128]{3,2,1,0:T(8,128)}), f32[8,2,8,128]{3,2,1,0:T(8,128)S(1)}, u32[]{:S(2)}, u32[]{:S(2)}) async-start(f32[8,2,8,128]{3,2,1,0:T(8,128)} %copy.56), calls=%async_computation | async-start | bytes 131072 | tf_op jit(solution)/shard_map/all_to_all | solution.py:99
  74.4 0.1 copy.59
  74.5 0.1 copy.65
  74.6 5.5 %all-to-all-done = f32[8,2,8,128]{3,2,1,0:T(8,128)S(1)} async-done(((f32[8,2,8,128]{3,2,1,0:T(8,128)}), f32[8,2,8,128]{3,2,1,0:T(8,128)S(1)}, u32[]{:S(2)}, u32[]{:S(2)}) %all-to-all-start) | async-done | bytes 65568 | tf_op jit(solution)/shard_map/all_to_all | solution.py:99
  80.0 0.1 fusion.14
  80.2 0.1 divide_convert_fusion
  80.3 1.0 collective-permute-start
  81.3 2.7 %collective-permute-done = bf16[2,2048]{1,0:T(2,128)(2,1)S(1)} collective-permute-done((bf16[2,2048]{1,0:T(2,128)(2,1)S(1)}, bf16[2,2048]{1,0:T(2,128)(2,1)S(1)}, u32[]{:S(2)}, u32[]{:S(2)}) %collective-permute-start) | collective-permute-done | bytes 8224 | tf_op jit(solution)/shard_map/ppermute | solution.py:18
  84.0 0.8 collective-permute-start.1
  84.9 0.0 copy-done.5
  84.9 0.6 dynamic-slice
  86.1 2.7 %collective-permute-done.1 = bf16[4,2048]{1,0:T(4,128)(2,1)S(1)} collective-permute-done((bf16[4,2048]{1,0:T(4,128)(2,1)S(1)}, bf16[4,2048]{1,0:T(4,128)(2,1)S(1)}, u32[]{:S(2)}, u32[]{:S(2)}) %collective-permute-start.1) | collective-permute-done | bytes 16416 | tf_op jit(solution)/shard_map/ppermute | solution.py:18
  88.8 4.6 %fusion.17 = f32[8,2048]{1,0:T(8,128)S(1)} fusion(bf16[2048,2048]{1,0:T(8,128)(2,1)} %param.12, bf16[4,2048]{1,0:T(4,128)(2,1)S(1)} %collective-permute-done.1, bf16[4,2048]{1,0:T(4,128)(2,1)S(1)} %maximum_select_fusion.2, pred[]{:T(512)S(6)} %eq.19), kind=kOutput, calls=%fused_computation.28 | convolution fusion | flops 67256320 | bytes 8486913 | tf_op jit(solution)/shard_map/dot_general | solution.py:113
  93.3 10.7 %all-reduce = bf16[8,2048]{1,0:T(8,128)(2,1)S(1)} all-reduce(f32[8,2048]{1,0:T(8,128)S(1)} %fusion.17), channel_id=2, replica_groups=mesh['group'=2,'lender'=4,'tensor'=4] {'tensor'}, use_global_device_ids=true, to_apply=%region_12.13.clone | all-reduce | flops 16384 | bytes 98304
  104.0 0.6 dynamic-slice_convert_fusion
  (21 shorter events, 0.2 us)
Async XLA Ops:
  6.5 44.5 %copy-start = (bf16[2,32,128,128]{3,2,1,0:T(8,128)(2,1)S(1)}, bf16[2,32,128,128]{3,2,1,0:T(8,128)(2,1)}, u32[]{:S(2)}) copy-start(bf16[2,32,128,128]{3,2,1,0:T(8,128)(2,1)} %param.13) | copy-start | bytes 6291460
  6.5 6.1 %copy-start.1 = (bf16[8,2048]{1,0:T(8,128)(2,1)S(1)}, bf16[8,2048]{1,0:T(8,128)(2,1)}, u32[]{:S(2)}) copy-start(bf16[8,2048]{1,0:T(8,128)(2,1)} %param.9) | copy-start | bytes 98308
  6.5 6.3 %copy-start.2 = (s32[8,2,16]{2,1,0:T(2,128)S(1)}, s32[8,2,16]{2,1,0:T(2,128)}, u32[]{:S(2)}) copy-start(s32[8,2,16]{2,1,0:T(2,128)} %param.15) | copy-start | bytes 3076
  6.5 6.4 %copy-start.3 = (s32[8,2]{0,1:T(2,128)S(1)}, s32[8,2]{0,1:T(2,128)}, u32[]{:S(2)}) copy-start(s32[8,2]{0,1:T(2,128)} %param.17) | copy-start | bytes 196
  6.5 6.5 %copy-start.4 = (s32[2,128]{1,0:T(2,128)S(1)}, s32[2,128]{1,0:T(2,128)}, u32[]{:S(2)}) copy-start(s32[2,128]{1,0:T(2,128)} %param.16) | copy-start | bytes 3076
  6.5 43.3 %all-reduce.3.cloned.1.call-start = ((), (), s32[]{:S(2)}) async-start(), calls=%async_computation.3 | async-start | bytes 131072 | tf_op jit(solution)/shard_map/psum | solution.py:49
  12.6 72.2 %copy-start.5 = (u32[32]{0:T(128)S(1)}, u32[32]{0:T(128)}, u32[]{:S(2)}) copy-start(u32[32]{0:T(128)} %constant.69) | copy-start | bytes 388
  53.3 9.0 %all-to-all-start.1 = ((f32[8,2,8]{2,1,0:T(2,128)}), f32[8,2,8]{2,1,0:T(2,128)S(1)}, u32[]{:S(2)}, u32[]{:S(2)}) async-start(f32[8,2,8]{2,1,0:T(2,128)} %copy.57), calls=%async_computation.1 | async-start | bytes 16384 | tf_op jit(solution)/shard_map/all_to_all | solution.py:97
  62.2 8.8 %all-to-all-start.2 = ((f32[8,2,8]{2,1,0:T(2,128)}), f32[8,2,8]{2,1,0:T(2,128)S(1)}, u32[]{:S(2)}, u32[]{:S(2)}) async-start(f32[8,2,8]{2,1,0:T(2,128)} %copy.63), calls=%async_computation.2 | async-start | bytes 16384 | tf_op jit(solution)/shard_map/all_to_all | solution.py:98
  71.0 9.0 %all-to-all-start = ((f32[8,2,8,128]{3,2,1,0:T(8,128)}), f32[8,2,8,128]{3,2,1,0:T(8,128)S(1)}, u32[]{:S(2)}, u32[]{:S(2)}) async-start(f32[8,2,8,128]{3,2,1,0:T(8,128)} %copy.56), calls=%async_computation | async-start | bytes 131072 | tf_op jit(solution)/shard_map/all_to_all | solution.py:99
  80.3 3.7 %collective-permute-start = (bf16[2,2048]{1,0:T(2,128)(2,1)S(1)}, bf16[2,2048]{1,0:T(2,128)(2,1)S(1)}, u32[]{:S(2)}, u32[]{:S(2)}) collective-permute-start(bf16[2,2048]{1,0:T(2,128)(2,1)S(1)} %bitcast.36), channel_id=1, source_target_pairs={{0,4},{4,0},{8,12},{12,8},{1,5},{5,1},{9,13},{13,9},{2,6},{6,2},{1... | collective-permute-start | bytes 24584 | tf_op jit(solution)/shard_map/ppermute | solution.py:18
  84.0 4.7 %collective-permute-start.1 = (bf16[4,2048]{1,0:T(4,128)(2,1)S(1)}, bf16[4,2048]{1,0:T(4,128)(2,1)S(1)}, u32[]{:S(2)}, u32[]{:S(2)}) collective-permute-start(bf16[4,2048]{1,0:T(4,128)(2,1)S(1)} %maximum_select_fusion.2), channel_id=1, source_target_pairs={{0,8},{4,12},{8,0},{12,4},{1,9},{5,13},{9,1},{13,5},{2,10},{6,14},... | collective-permute-start | bytes 49160 | tf_op jit(solution)/shard_map/ppermute | solution.py:18
Sparse Core Ops, SparseCore 0:
  12.8 37.0 all-reduce.2
